TPU v7x, 512 devices: a whole 4x4x16 slice. The times are simulated.
512 devices in a mesh: cluster: 64 (over y, z), member: 8 (over x, core).
Axes of the slice: x: 4, y: 4, z: 16, core: 2. Of those that a mesh axis runs over, the one named last changes fastest.
Arguments:
- leaf_centers: float32 [3, 512], replicated, may hold values from 0 to 1
- source_coords: float32 [3, 65536], P(None, ('cluster', 'member')), may hold values from -1 to 1
- target_points: float32 [3, 65536], P(None, ('cluster', 'member')), may hold values from 0 to 1
- charges: float32 [8, 65536], P(None, ('cluster', 'member')), may hold values from -6 to 6
- boundary_data: float32 [8, 65536], P(None, ('cluster', 'member')), may hold values from -6 to 6
- step_sizes: float32 [8], replicated, may hold values from 0.2 to 1
- valid_count: int32 [512], P(('cluster', 'member')), may hold values from 64 to 128, as said below
- near_lists: int32 [64, 26], replicated, may hold values from 0 to 63, as said below
Outputs:
- new_charges: float32 [8, 65536], P(None, ('cluster', 'member'))
- residual: float32 [8, 65536], P(None, ('cluster', 'member'))
Inputs may be any that keep to these rules, and one draw needn't show every extreme that they name: `valid_count`: some leaf has 128 live slots and some has half of 128. `near_lists`: row c names 26 different clusters, none of them c.
All inputs are finite; a program needn't handle non-finite values.
Results may differ from a plain program's by a relative error of at most 0.0003.
Values sent between devices are 32-bit elements; how exact they have to be, the bound alone decides.
No kernel may reach another device: no remote copies, remote signals or barrier semaphores. Data moves between devices by JAX's collectives and lax.ppermute only.
A program may use at most 64 MiB of HBM per device.

v0:
```python
import math
import jax
import jax.numpy as jnp
import numpy as np
from jax import lax
from jax.sharding import PartitionSpec as P

ITERS = 2
HALF_SIDE = 0.08
SOFTENING = 0.0025


def cheby_nodes(number):
    return np.cos(np.pi * (2 * np.arange(number) + 1) / (2 * number))


def basis_line(coord, number):
    nodes = cheby_nodes(number)
    factors = []
    for first in range(number):
        factor = jnp.ones_like(coord)
        for other in range(number):
            if other != first:
                factor = factor * (coord - nodes[other]) / (nodes[first] - nodes[other])
        factors.append(factor)
    return jnp.stack(factors, 0)


def lagrange(coords):
    along_x = basis_line(coords[0], 2)
    along_y = basis_line(coords[1], 4)
    along_z = basis_line(coords[2], 4)
    joined = along_x[:, None, None, :] * along_y[None, :, None, :] * along_z[None, None, :, :]
    return joined.reshape(32, coords.shape[1])


def proxy_grid():
    grid_x, grid_y, grid_z = np.meshgrid(
        cheby_nodes(2), cheby_nodes(4), cheby_nodes(4), indexing="ij"
    )
    return jnp.asarray(
        np.stack([grid_x.reshape(-1), grid_y.reshape(-1), grid_z.reshape(-1)], 0), jnp.float32
    )


def potential(targets, sources, weights):
    target_count = targets.shape[1]
    source_count = sources.shape[1]
    limit = max(128, (1 << 20) // target_count)
    src_block = math.gcd(source_count, limit)

    def advance(turn, running):
        pts = lax.dynamic_slice_in_dim(sources, turn * src_block, src_block, 1)
        wts = lax.dynamic_slice_in_dim(weights, turn * src_block, src_block, 1)
        distance = (pts[0][:, None] - targets[0][None, :]) ** 2
        distance = distance + (pts[1][:, None] - targets[1][None, :]) ** 2
        distance = distance + (pts[2][:, None] - targets[2][None, :]) ** 2
        kernel = lax.rsqrt(distance + SOFTENING)
        return running + jnp.dot(
            wts, kernel, precision=lax.Precision.HIGHEST, preferred_element_type=jnp.float32
        )

    start_value = jnp.zeros((weights.shape[0], target_count), jnp.float32)
    return lax.fori_loop(0, source_count // src_block, advance, start_value)


def flatten_packets(packets):
    return jnp.moveaxis(packets, 1, 0).reshape(packets.shape[1], -1)


def body(
    leaf_centers,
    source_coords,
    target_points,
    charges,
    boundary_data,
    step_sizes,
    valid_count,
    near_lists,
):
    clusters = lax.axis_size("cluster")
    members = lax.axis_size("member")
    leaf_size = source_coords.shape[1]
    proxies = 32
    cluster_index = lax.axis_index("cluster")
    member_index = lax.axis_index("member")
    leaf_index = cluster_index * members + member_index
    center = lax.dynamic_slice_in_dim(leaf_centers, leaf_index, 1, 1)
    source_points = center + HALF_SIDE * source_coords
    live = (jnp.arange(leaf_size, dtype=jnp.int32) < valid_count[0]).astype(jnp.float32)
    interp = lagrange(source_coords)
    offsets = proxy_grid()
    proxy_points = leaf_centers[:, :, None] + HALF_SIDE * offsets[:, None, :]
    my_near = lax.dynamic_index_in_dim(near_lists, cluster_index, 0, keepdims=False)
    listed = jnp.any(near_lists == cluster_index, axis=1)
    own_near = jnp.concatenate([jnp.reshape(cluster_index, (1,)), my_near])
    cluster_ids = jnp.arange(clusters, dtype=jnp.int32)
    far_cluster = jnp.all(cluster_ids[:, None] != own_near[None, :], axis=1).astype(jnp.float32)
    scale = 1.0 / math.sqrt(clusters * members * leaf_size)

    def outgoing(packet):
        return jnp.where(listed[:, None, None], packet[None], jnp.zeros_like(packet)[None])

    def select(received, own_piece):
        return jnp.concatenate([own_piece[None], jnp.take(received, my_near, axis=0)], 0)

    arrived_points = lax.all_to_all(
        outgoing(source_points), "cluster", split_axis=0, concat_axis=0, tiled=True
    )
    near_points = select(arrived_points, source_points)
    all_near_points = lax.all_gather(near_points, "member", axis=0, tiled=True)
    every_far = jnp.repeat(far_cluster, members * proxies)
    every_proxy = proxy_points.reshape(3, -1)
    current = charges * live
    residual = current
    for turn in range(ITERS):
        proxy_charges = jnp.einsum("fj,pj->fp", current, interp, precision=lax.Precision.HIGHEST)
        arrived_charges = lax.all_to_all(
            outgoing(current), "cluster", split_axis=0, concat_axis=0, tiled=True
        )
        near_charges = select(arrived_charges, current)
        near_sum = potential(
            target_points,
            flatten_packets(all_near_points),
            flatten_packets(lax.all_gather(near_charges, "member", axis=0, tiled=True)),
        )
        piece = lax.all_gather(proxy_charges, ("cluster", "member"), axis=1, tiled=True)
        positions = lax.slice_in_dim(every_proxy, 0, piece.shape[1], axis=1)
        far_sum = potential(target_points, positions, piece * every_far[None, :])
        field_sum = near_sum + far_sum
        residual = live * (boundary_data - scale * field_sum)
        current = live * (current + step_sizes[:, None] * residual / (1.0 + jnp.abs(residual)))
    return (current, residual)


def solution(mesh):
    in_specs = (
        P(),
        P(None, ("cluster", "member")),
        P(None, ("cluster", "member")),
        P(None, ("cluster", "member")),
        P(None, ("cluster", "member")),
        P(),
        P(("cluster", "member")),
        P(),
    )
    out_specs = (P(None, ("cluster", "member")), P(None, ("cluster", "member")))
    return jax.shard_map(body, mesh=mesh, in_specs=in_specs, out_specs=out_specs, check_vma=False)
```

profile of v0, /device:TPU:1, one launch (start us, length us, event | category | flops | bytes accessed | tf_op | source)
XLA Modules:
  0.0 408.0 jit_solution(5029262380854414042)
XLA Ops:
  1.4 0.9 dynamic-slice_reduce_fusion.1
  3.0 0.8 broadcast_select_fusion.2
  3.8 19.3 %all-to-all-start.1 = ((f32[64,3,128]{2,1,0:T(4,128)}), f32[64,3,128]{2,1,0:T(4,128)S(1)}, u32[]{:S(2)}, u32[]{:S(2)}) async-start(f32[64,3,128]{2,1,0:T(4,128)} %broadcast_select_fusion.2), calls=%async_computation.1 | async-start | bytes 262144 | tf_op jit(solution)/shard_map/all_to_all | solution.py:107
  23.1 0.9 dynamic-slice_reduce_fusion
  24.0 0.8 add_multiply_fusion.3
  26.4 117.8 %all-gather = f32[512,32,8]{1,2,0:T(8,128)S(1)} all-gather(f32[1,32,8]{1,2,0:T(8,128)S(1)} %convolution_bitcast_fusion.1), channel_id=1, replica_groups=mesh['cluster'=64,'member'=8] {'cluster','member'}, dimensions={0}, use_global_device_ids=true | all-gather | bytes 525312 | tf_op jit(solution)/shard_map/all_gather | solution.py:127
  144.5 1.0 reshape.131
  146.6 10.0 %while.57 = (s32[]{:T(128)}, f32[8,128]{1,0:T(8,128)S(1)}, f32[8,16384]{1,0:T(8,128)S(1)}, f32[3,16384]{1,0:T(4,128)S(1)}, f32[3,128]{1,0:T(4,128)S(1)}, /*index...) while((s32[]{:T(128)}, f32[8,128]{1,0:T(8,128)S(1)}, ...), condition=%wide.region_5.7_spmd.clone, body=%wide.region_4.6_spmd.clone.sunk | while | flops 110102536 | bytes 570069 | solution.py:64
  146.9 4.8 %fusion.110 = f32[8,128]{1,0:T(8,128)S(1)} fusion(f32[128]{0:T(128)S(1)} %get-tuple-element.677, f32[8192]{0:T(1024)S(1)} %bitcast.113, f32[128]{0:T(128)S(1)} %get-tuple-element.679, f32[8192]{0:T(1024)S(1)} %bitcast.112, f32[128]{0:T(128)S(1)} %get-tuple-element.681, f32[8192]{0:T(1024)S(1)} %bitcast.111, f32[8,16384]{1,0:T(8,128)S(1)} %get-tuple-element.762, ...), kind=kOutput, calls=%fused_computation.46.clone.1 | convolution fusion | flops 110102528 | bytes 370181 | tf_op jit(solution)/shard_map/while/body/eval_jaxpr/dot_general | solution.py:59
  151.9 4.8 %fusion.110 = f32[8,128]{1,0:T(8,128)S(1)} fusion(f32[128]{0:T(128)S(1)} %get-tuple-element.677, f32[8192]{0:T(1024)S(1)} %bitcast.113, f32[128]{0:T(128)S(1)} %get-tuple-element.679, f32[8192]{0:T(1024)S(1)} %bitcast.112, f32[128]{0:T(128)S(1)} %get-tuple-element.681, f32[8192]{0:T(1024)S(1)} %bitcast.111, f32[8,16384]{1,0:T(8,128)S(1)} %get-tuple-element.762, ...), kind=kOutput, calls=%fused_computation.46.clone.1 | convolution fusion | flops 110102528 | bytes 370181 | tf_op jit(solution)/shard_map/while/body/eval_jaxpr/dot_general | solution.py:59
  156.7 0.8 broadcast_select_fusion.1
  157.6 11.6 %all-to-all-start = ((f32[64,8,128]{2,1,0:T(8,128)}), f32[64,8,128]{2,1,0:T(8,128)S(1)}, u32[]{:S(2)}, u32[]{:S(2)}) async-start(f32[64,8,128]{2,1,0:T(8,128)} %broadcast_select_fusion.1), calls=%async_computation | async-start | bytes 524288 | tf_op jit(solution)/shard_map/all_to_all | solution.py:118
  170.0 13.3 %all_gather.16 = f32[216,3,128]{2,1,0:T(4,128)S(1)} all-gather(f32[27,3,128]{2,1,0:T(4,128)S(1)} %pad_maximum_fusion.2), channel_id=1, replica_groups=mesh['cluster'=64,'member'=8] {'member'}, dimensions={0}, use_global_device_ids=true | all-gather | bytes 373248 | tf_op jit(solution)/shard_map/all_gather | solution.py:111
  183.3 5.9 %all-to-all-done = f32[64,8,128]{2,1,0:T(8,128)S(1)} async-done(((f32[64,8,128]{2,1,0:T(8,128)}), f32[64,8,128]{2,1,0:T(8,128)S(1)}, u32[]{:S(2)}, u32[]{:S(2)}) %all-to-all-start) | async-done | bytes 262176 | tf_op jit(solution)/shard_map/all_to_all | solution.py:118
  189.9 15.3 %all_gather.15 = f32[216,8,128]{2,1,0:T(8,128)S(1)} all-gather(f32[27,8,128]{2,1,0:T(8,128)S(1)} %pad_maximum_fusion), channel_id=1, replica_groups=mesh['cluster'=64,'member'=8] {'member'}, dimensions={0}, use_global_device_ids=true | all-gather | bytes 995328 | tf_op jit(solution)/shard_map/all_gather | solution.py:125
  205.2 23.9 %while.56 = (s32[]{:T(128)}, f32[8,128]{1,0:T(8,128)S(1)}, f32[8,27648]{1,0:T(8,128)S(1)}, f32[3,27648]{1,0:T(4,128)S(1)}, f32[3,128]{1,0:T(4,128)S(1)}, /*index...) while((s32[]{:T(128)}, f32[8,128]{1,0:T(8,128)S(1)}, ...), condition=%wide.region_2.4_spmd.clone, body=%wide.region_1.0_spmd.clone.sunk | while | flops 13764617 | bytes 82645 | solution.py:64
  205.3 0.8 convolution_add_fusion.4
  206.2 0.8 convolution_add_fusion.4
  207.0 0.8 convolution_add_fusion.4
  207.9 0.8 convolution_add_fusion.4
  208.8 0.8 convolution_add_fusion.4
  209.7 0.8 convolution_add_fusion.4
  210.6 0.8 convolution_add_fusion.4
  211.5 0.8 convolution_add_fusion.4
  212.4 0.8 convolution_add_fusion.4
  213.2 0.8 convolution_add_fusion.4
  214.1 0.8 convolution_add_fusion.4
  215.0 0.8 convolution_add_fusion.4
  215.9 0.8 convolution_add_fusion.4
  216.8 0.8 convolution_add_fusion.4
  217.7 0.8 convolution_add_fusion.4
  218.5 0.8 convolution_add_fusion.4
  219.4 0.8 convolution_add_fusion.4
  220.3 0.8 convolution_add_fusion.4
  221.2 0.8 convolution_add_fusion.4
  222.1 0.8 convolution_add_fusion.4
  223.0 0.8 convolution_add_fusion.4
  223.9 0.8 convolution_add_fusion.4
  224.7 0.8 convolution_add_fusion.4
  225.6 0.8 convolution_add_fusion.4
  226.5 0.8 convolution_add_fusion.4
  227.4 0.8 convolution_add_fusion.4
  228.3 0.8 convolution_add_fusion.4
  229.1 0.8 broadcast_select_fusion
  230.1 7.5 %all-to-all-start.2 = ((f32[64,8,128]{2,1,0:T(8,128)}), f32[64,8,128]{2,1,0:T(8,128)}, u32[]{:S(2)}, u32[]{:S(2)}) async-start(f32[64,8,128]{2,1,0:T(8,128)} %broadcast_select_fusion), calls=%async_computation.2 | async-start | bytes 524288 | tf_op jit(solution)/shard_map/all_to_all | solution.py:118
  237.6 119.2 %all-gather.1 = f32[512,32,8]{1,2,0:T(8,128)S(1)} all-gather(f32[1,32,8]{1,2,0:T(8,128)S(1)} %convolution_bitcast_fusion), channel_id=1, replica_groups=mesh['cluster'=64,'member'=8] {'cluster','member'}, dimensions={0}, use_global_device_ids=true | all-gather | bytes 525312 | tf_op jit(solution)/shard_map/all_gather | solution.py:127
  357.2 1.0 reshape.133
  358.2 10.0 %while.59 = (s32[]{:T(128)}, f32[8,128]{1,0:T(8,128)S(1)}, f32[8,16384]{1,0:T(8,128)S(1)}, f32[3,16384]{1,0:T(4,128)S(1)}, f32[3,128]{1,0:T(4,128)S(1)}, /*index...) while((s32[]{:T(128)}, f32[8,128]{1,0:T(8,128)S(1)}, ...), condition=%wide.region_9.11_spmd.clone, body=%wide.region_8.10_spmd.clone.sunk | while | flops 110102536 | bytes 570069 | solution.py:64
  358.5 4.8 %fusion.115 = f32[8,128]{1,0:T(8,128)S(1)} fusion(f32[128]{0:T(128)S(1)} %get-tuple-element.699, f32[8192]{0:T(1024)S(1)} %bitcast.116, f32[128]{0:T(128)S(1)} %get-tuple-element.701, f32[8192]{0:T(1024)S(1)} %bitcast.115, f32[128]{0:T(128)S(1)} %get-tuple-element.703, f32[8192]{0:T(1024)S(1)} %bitcast.114, f32[8,16384]{1,0:T(8,128)S(1)} %get-tuple-element.828, ...), kind=kOutput, calls=%fused_computation.97.clone.1 | convolution fusion | flops 110102528 | bytes 370181 | tf_op jit(solution)/shard_map/while/body/eval_jaxpr/dot_general | solution.py:59
  363.5 4.8 %fusion.115 = f32[8,128]{1,0:T(8,128)S(1)} fusion(f32[128]{0:T(128)S(1)} %get-tuple-element.699, f32[8192]{0:T(1024)S(1)} %bitcast.116, f32[128]{0:T(128)S(1)} %get-tuple-element.701, f32[8192]{0:T(1024)S(1)} %bitcast.115, f32[128]{0:T(128)S(1)} %get-tuple-element.703, f32[8192]{0:T(1024)S(1)} %bitcast.114, f32[8,16384]{1,0:T(8,128)S(1)} %get-tuple-element.828, ...), kind=kOutput, calls=%fused_computation.97.clone.1 | convolution fusion | flops 110102528 | bytes 370181 | tf_op jit(solution)/shard_map/while/body/eval_jaxpr/dot_general | solution.py:59
  368.3 1.5 gather_fusion.2
  369.9 13.5 %all_gather.18 = f32[216,8,128]{2,1,0:T(8,128)S(1)} all-gather(f32[27,8,128]{2,1,0:T(8,128)S(1)} %pad_maximum_fusion.1), channel_id=1, replica_groups=mesh['cluster'=64,'member'=8] {'member'}, dimensions={0}, use_global_device_ids=true | all-gather | bytes 995328 | tf_op jit(solution)/shard_map/all_gather | solution.py:125
  383.4 23.9 %while.58 = (s32[]{:T(128)}, f32[8,128]{1,0:T(8,128)S(1)}, f32[8,27648]{1,0:T(8,128)S(1)}, f32[3,27648]{1,0:T(4,128)S(1)}, f32[3,128]{1,0:T(4,128)S(1)}, /*index...) while((s32[]{:T(128)}, f32[8,128]{1,0:T(8,128)S(1)}, ...), condition=%wide.region_7.9_spmd.clone, body=%wide.region_6.8_spmd.clone.sunk | while | flops 13764617 | bytes 82645 | solution.py:64
  384.4 0.8 convolution_add_fusion.5
  385.3 0.8 convolution_add_fusion.5
  386.2 0.8 convolution_add_fusion.5
  390.6 0.8 convolution_add_fusion.5
  391.5 0.8 convolution_add_fusion.5
  395.9 0.8 convolution_add_fusion.5
  396.8 0.8 convolution_add_fusion.5
  397.7 0.8 convolution_add_fusion.5
  401.2 0.8 convolution_add_fusion.5
  402.1 0.8 convolution_add_fusion.5
  403.0 0.8 convolution_add_fusion.5
  (190 shorter events, 24.8 us)
Async XLA Ops:
  3.8 153.8 %all-to-all-start.1 = ((f32[64,3,128]{2,1,0:T(4,128)}), f32[64,3,128]{2,1,0:T(4,128)S(1)}, u32[]{:S(2)}, u32[]{:S(2)}) async-start(f32[64,3,128]{2,1,0:T(4,128)} %broadcast_select_fusion.2), calls=%async_computation.1 | async-start | bytes 262144 | tf_op jit(solution)/shard_map/all_to_all | solution.py:107
  144.5 1.3 copy-start.4
  144.5 1.3 copy-start.5
  145.5 1.1 copy-start
  146.6 22.6 %copy-start.3 = (f32[3,128]{1,0:T(4,128)S(1)}, f32[3,128]{1,0:T(4,128)}, u32[]{:S(2)}) copy-start(f32[3,128]{1,0:T(4,128)} %param.20) | copy-start | bytes 4612
  146.6 22.6 %copy-start.1 = (f32[8,128]{1,0:T(8,128)S(1)}, f32[8,128]{1,0:T(8,128)}, u32[]{:S(2)}) copy-start(f32[8,128]{1,0:T(8,128)} %param.22) | copy-start | bytes 12292
  157.6 31.7 %all-to-all-start = ((f32[64,8,128]{2,1,0:T(8,128)}), f32[64,8,128]{2,1,0:T(8,128)S(1)}, u32[]{:S(2)}, u32[]{:S(2)}) async-start(f32[64,8,128]{2,1,0:T(8,128)} %broadcast_select_fusion.1), calls=%async_computation | async-start | bytes 524288 | tf_op jit(solution)/shard_map/all_to_all | solution.py:118
  205.2 23.9 %copy-start.2 = (f32[8,128]{1,0:T(8,128)S(1)}, f32[8,128]{1,0:T(8,128)}, u32[]{:S(2)}) copy-start(f32[8,128]{1,0:T(8,128)} %param.23) | copy-start | bytes 12292
  205.2 23.9 %copy-start.6 = (f32[8]{0:T(128)S(1)}, f32[8]{0:T(128)}, u32[]{:S(2)}) copy-start(f32[8]{0:T(128)} %param.24) | copy-start | bytes 100
  230.1 138.2 %all-to-all-start.2 = ((f32[64,8,128]{2,1,0:T(8,128)}), f32[64,8,128]{2,1,0:T(8,128)}, u32[]{:S(2)}, u32[]{:S(2)}) async-start(f32[64,8,128]{2,1,0:T(8,128)} %broadcast_select_fusion), calls=%async_computation.2 | async-start | bytes 524288 | tf_op jit(solution)/shard_map/all_to_all | solution.py:118
where the time goes:
time: 409 us; the launch traced here: 408 us
  blocking collectives  279 us (68%)
  matrix products  60.2 us (15%)
  starting transfers between devices  38.4 us (9%)
  local copies, waits for them, and re-layouts  13.7 us (3%)
  other arithmetic  7.24 us (2%)
  waiting for transfers between devices  5.93 us (1%)
    all_gather x2, blocking collectives, body(): lax.all_gather(proxy_charges, ('cluster', 'member'), axis=1, tiled=True)  237 us
    dot_general x58, matrix products, advance(): jnp.dot(wts, kernel, precision=lax.Precision.HIGHEST, preferred_element_t...  60 us
    all_gather x2, blocking collectives, body(): lax.all_gather(near_charges, 'member', axis=0, tiled=True)  28.7 us
    all_to_all x1, starting transfers between devices, body(): lax.all_to_all(outgoing(source_points), 'cluster', split_axis=0, concat_a...  19.3 us
    all_to_all x2, starting transfers between devices, body(): lax.all_to_all(outgoing(current), 'cluster', split_axis=0, concat_axis=0,...  19.1 us
    all_gather x1, blocking collectives, body(): all_near_points = lax.all_gather(near_points, 'member', axis=0, tiled=True)  13.3 us
  transfers between devices with their start and end apart: 3, of which 1 were waited for; matrix products, arithmetic and copies ran while one was open for 7% of the time, Pallas kernels for 0%

commit v1 on v0

--- a/solution.py
+++ b/solution.py
@@ -124,7 +124,15 @@
             flatten_packets(all_near_points),
             flatten_packets(lax.all_gather(near_charges, "member", axis=0, tiled=True)),
         )
-        piece = lax.all_gather(proxy_charges, ("cluster", "member"), axis=1, tiled=True)
+        piece = jnp.concatenate(
+            lax.all_to_all(
+                jnp.stack([proxy_charges] * lax.axis_size(("cluster", "member"))),
+                ("cluster", "member"),
+                0,
+                0,
+            ),
+            axis=1,
+        )
         positions = lax.slice_in_dim(every_proxy, 0, piece.shape[1], axis=1)
         far_sum = potential(target_points, positions, piece * every_far[None, :])
         field_sum = near_sum + far_sum

time: 409 us -> 249 us (0.61)
  blocking collectives: 279 us -> 51.5 us
  starting transfers between devices: 38.4 us -> 67.6 us
  waiting for transfers between devices: 5.93 us -> 27.9 us
  local copies, waits for them, and re-layouts: 13.7 us -> 24.5 us
  other arithmetic: 7.24 us -> 12.3 us
    all_gather x2 -> x0, blocking collectives: 237 us -> none  [body(): lax.all_gather(proxy_charges, ('cluster', 'member'), axis=1, tiled=True)]
    all_to_all x0 -> x2, starting transfers between devices: none -> 27.4 us  [body(): lax.all_to_all(jnp.stack([proxy_charges] * lax.axis_size(('cluster', 'mem...]
    all_to_all x2, waiting for transfers between devices: 5.93 us -> 21.4 us  [body(): lax.all_to_all(outgoing(current), 'cluster', split_axis=0, concat_axis=0,...]
    reshape x0 -> x4, local copies, waits for them, and re-layouts: none -> 8.54 us  [body(): jnp.concatenate(lax.all_to_all(jnp.stack([proxy_charges] * lax.axis_size(...]
    all_gather x2, blocking collectives: 28.7 us -> 36.7 us  [body(): lax.all_gather(near_charges, 'member', axis=0, tiled=True)]
    all_to_all x1, waiting for transfers between devices: 0.01 us -> 6.48 us  [body(): lax.all_to_all(outgoing(source_points), 'cluster', split_axis=0, concat_a...]
  transfers between devices with their start and end apart: 3 -> 5, of which waited for: 1 -> 3; matrix products, arithmetic and copies ran while one was open for 7% -> 23% of each run, Pallas kernels for 0% -> 0%
where the time goes in v1:
time: 249 us; the launch traced here: 248 us
  starting transfers between devices  67.6 us (27%)
  matrix products  60.2 us (24%)
  blocking collectives  51.5 us (21%)
  waiting for transfers between devices  27.9 us (11%)
  local copies, waits for them, and re-layouts  24.5 us (10%)
  other arithmetic  12.3 us (5%)
    dot_general x58, matrix products, advance(): jnp.dot(wts, kernel, precision=lax.Precision.HIGHEST, preferred_element_t...  60 us
    all_gather x2, blocking collectives, body(): lax.all_gather(near_charges, 'member', axis=0, tiled=True)  36.7 us
    all_to_all x2, starting transfers between devices, body(): lax.all_to_all(jnp.stack([proxy_charges] * lax.axis_size(('cluster', 'mem...  27.4 us
    all_to_all x2, waiting for transfers between devices, body(): lax.all_to_all(outgoing(current), 'cluster', split_axis=0, concat_axis=0,...  21.4 us
    all_to_all x2, starting transfers between devices, body(): lax.all_to_all(outgoing(current), 'cluster', split_axis=0, concat_axis=0,...  21 us
    all_to_all x1, starting transfers between devices, body(): lax.all_to_all(outgoing(source_points), 'cluster', split_axis=0, concat_a...  19.3 us
    all_gather x1, blocking collectives, body(): all_near_points = lax.all_gather(near_points, 'member', axis=0, tiled=True)  14.7 us
    reshape x4, local copies, waits for them, and re-layouts, body(): jnp.concatenate(lax.all_to_all(jnp.stack([proxy_charges] * lax.axis_size(...  8.54 us
  transfers between devices with their start and end apart: 5, of which 3 were waited for; matrix products, arithmetic and copies ran while one was open for 23% of the time, Pallas kernels for 0%

profile of v1, /device:TPU:1, one launch (start us, length us, event | category | flops | bytes accessed | tf_op | source)
XLA Modules:
  0.0 247.7 jit_solution(14835722752383558613)
XLA Ops:
  1.4 0.9 dynamic-slice_reduce_fusion.1
  3.0 0.8 broadcast_select_fusion.2
  3.8 19.3 %all-to-all-start.1 = ((f32[64,3,128]{2,1,0:T(4,128)}), f32[64,3,128]{2,1,0:T(4,128)S(1)}, u32[]{:S(2)}, u32[]{:S(2)}) async-start(f32[64,3,128]{2,1,0:T(4,128)} %broadcast_select_fusion.2), calls=%async_computation.1 | async-start | bytes 262144 | tf_op jit(solution)/shard_map/all_to_all | solution.py:107
  23.1 0.9 dynamic-slice_reduce_fusion
  24.0 0.8 add_multiply_fusion.3
  25.7 1.0 broadcast_add_fusion
  27.8 1.7 reshape.157
  30.0 0.8 broadcast_select_fusion.1
  30.9 6.5 %all-to-all-done.1 = f32[64,3,128]{2,1,0:T(4,128)S(1)} async-done(((f32[64,3,128]{2,1,0:T(4,128)}), f32[64,3,128]{2,1,0:T(4,128)S(1)}, u32[]{:S(2)}, u32[]{:S(2)}) %all-to-all-start.1) | async-done | bytes 98336 | tf_op jit(solution)/shard_map/all_to_all | solution.py:107
  37.3 8.1 %all-to-all-start = ((f32[64,8,128]{2,1,0:T(8,128)}), f32[64,8,128]{2,1,0:T(8,128)S(1)}, u32[]{:S(2)}, u32[]{:S(2)}) async-start(f32[64,8,128]{2,1,0:T(8,128)} %broadcast_select_fusion.1), calls=%async_computation | async-start | bytes 524288 | tf_op jit(solution)/shard_map/all_to_all | solution.py:118
  46.3 14.7 %all_gather.10 = f32[216,3,128]{2,1,0:T(4,128)S(1)} all-gather(f32[27,3,128]{2,1,0:T(4,128)S(1)} %pad_maximum_fusion.2), channel_id=1, replica_groups=mesh['cluster'=64,'member'=8] {'member'}, dimensions={0}, use_global_device_ids=true | all-gather | bytes 373248 | tf_op jit(solution)/shard_map/all_gather | solution.py:111
  61.0 3.2 %all-to-all-done = f32[64,8,128]{2,1,0:T(8,128)S(1)} async-done(((f32[64,8,128]{2,1,0:T(8,128)}), f32[64,8,128]{2,1,0:T(8,128)S(1)}, u32[]{:S(2)}, u32[]{:S(2)}) %all-to-all-start) | async-done | bytes 262176 | tf_op jit(solution)/shard_map/all_to_all | solution.py:118
  64.2 15.5 %all-to-all-start.2 = ((f32[512,1,256]{2,1,0:T(1,128)}), f32[512,1,256]{2,1,0:T(1,128)S(1)}, u32[]{:S(2)}, u32[]{:S(2)}) async-start(f32[512,1,256]{2,1,0:T(1,128)} %reshape.157), calls=%async_computation.2 | async-start | bytes 1048576 | tf_op jit(solution)/shard_map/all_to_all | solution.py:128
  80.3 0.8 broadcast_select_fusion.4
  81.1 18.5 %all_gather.9 = f32[216,8,128]{2,1,0:T(8,128)S(1)} all-gather(f32[27,8,128]{2,1,0:T(8,128)S(1)} %pad_maximum_fusion), channel_id=1, replica_groups=mesh['cluster'=64,'member'=8] {'member'}, dimensions={0}, use_global_device_ids=true | all-gather | bytes 995328 | tf_op jit(solution)/shard_map/all_gather | solution.py:125
  99.7 23.9 %while.56 = (s32[]{:T(128)}, f32[8,128]{1,0:T(8,128)S(1)}, f32[8,27648]{1,0:T(8,128)S(1)}, f32[3,27648]{1,0:T(4,128)S(1)}, f32[3,128]{1,0:T(4,128)S(1)}, /*index...) while((s32[]{:T(128)}, f32[8,128]{1,0:T(8,128)S(1)}, ...), condition=%wide.region_2.4_spmd.clone, body=%wide.region_1.0_spmd.clone.sunk | while | flops 13764617 | bytes 82645 | solution.py:64
  99.8 0.8 convolution_add_fusion.4
  100.7 0.8 convolution_add_fusion.4
  101.6 0.8 convolution_add_fusion.4
  102.5 0.8 convolution_add_fusion.4
  103.3 0.8 convolution_add_fusion.4
  104.2 0.8 convolution_add_fusion.4
  105.1 0.8 convolution_add_fusion.4
  106.0 0.8 convolution_add_fusion.4
  106.9 0.8 convolution_add_fusion.4
  109.5 0.8 convolution_add_fusion.4
  110.4 0.8 convolution_add_fusion.4
  111.3 0.8 convolution_add_fusion.4
  114.8 0.8 convolution_add_fusion.4
  115.7 0.8 convolution_add_fusion.4
  116.6 0.8 convolution_add_fusion.4
  121.0 0.8 convolution_add_fusion.4
  121.9 0.8 convolution_add_fusion.4
  124.8 1.9 reduce.5
  127.1 1.7 copy.14
  128.8 2.6 %reshape.119 = f32[8,16384]{1,0:T(8,128)S(1)} reshape(f32[8,512,32]{2,1,0:T(8,128)} %copy.14) | data formatting | bytes 1048576 | tf_op jit(solution)/shard_map/reshape | solution.py:127
  131.5 10.0 %while.57 = (s32[]{:T(128)}, f32[8,128]{1,0:T(8,128)S(1)}, f32[8,16384]{1,0:T(8,128)S(1)}, f32[3,16384]{1,0:T(4,128)S(1)}, f32[3,128]{1,0:T(4,128)S(1)}, /*index...) while((s32[]{:T(128)}, f32[8,128]{1,0:T(8,128)S(1)}, ...), condition=%wide.region_5.7_spmd.clone, body=%wide.region_4.6_spmd.clone.sunk | while | flops 110102536 | bytes 570069 | solution.py:64
  131.7 4.8 %fusion.112 = f32[8,128]{1,0:T(8,128)S(1)} fusion(f32[128]{0:T(128)S(1)} %get-tuple-element.677, f32[8192]{0:T(1024)S(1)} %bitcast.105, f32[128]{0:T(128)S(1)} %get-tuple-element.679, f32[8192]{0:T(1024)S(1)} %bitcast.104, f32[128]{0:T(128)S(1)} %get-tuple-element.681, f32[8192]{0:T(1024)S(1)} %bitcast.103, f32[8,16384]{1,0:T(8,128)S(1)} %get-tuple-element.762, ...), kind=kOutput, calls=%fused_computation.46.clone.1 | convolution fusion | flops 110102528 | bytes 370181 | tf_op jit(solution)/shard_map/while/body/eval_jaxpr/dot_general | solution.py:59
  136.7 4.8 %fusion.112 = f32[8,128]{1,0:T(8,128)S(1)} fusion(f32[128]{0:T(128)S(1)} %get-tuple-element.677, f32[8192]{0:T(1024)S(1)} %bitcast.105, f32[128]{0:T(128)S(1)} %get-tuple-element.679, f32[8192]{0:T(1024)S(1)} %bitcast.104, f32[128]{0:T(128)S(1)} %get-tuple-element.681, f32[8192]{0:T(1024)S(1)} %bitcast.103, f32[8,16384]{1,0:T(8,128)S(1)} %get-tuple-element.762, ...), kind=kOutput, calls=%fused_computation.46.clone.1 | convolution fusion | flops 110102528 | bytes 370181 | tf_op jit(solution)/shard_map/while/body/eval_jaxpr/dot_general | solution.py:59
  141.6 0.8 broadcast_select_fusion
  142.5 12.9 %all-to-all-start.3 = ((f32[64,8,128]{2,1,0:T(8,128)}), f32[64,8,128]{2,1,0:T(8,128)S(1)}, u32[]{:S(2)}, u32[]{:S(2)}) async-start(f32[64,8,128]{2,1,0:T(8,128)} %broadcast_select_fusion), calls=%async_computation.3 | async-start | bytes 524288 | tf_op jit(solution)/shard_map/all_to_all | solution.py:118
  155.7 1.7 reshape.159
  157.4 18.1 %all-to-all-done.3 = f32[64,8,128]{2,1,0:T(8,128)S(1)} async-done(((f32[64,8,128]{2,1,0:T(8,128)}), f32[64,8,128]{2,1,0:T(8,128)S(1)}, u32[]{:S(2)}, u32[]{:S(2)}) %all-to-all-start.3) | async-done | bytes 262176 | tf_op jit(solution)/shard_map/all_to_all | solution.py:118
  175.6 11.9 %all-to-all-start.4 = ((f32[512,1,256]{2,1,0:T(1,128)}), f32[512,1,256]{2,1,0:T(1,128)S(1)}, u32[]{:S(2)}, u32[]{:S(2)}) async-start(f32[512,1,256]{2,1,0:T(1,128)} %reshape.159), calls=%async_computation.4 | async-start | bytes 1048576 | tf_op jit(solution)/shard_map/all_to_all | solution.py:128
  188.3 18.2 %all_gather.11 = f32[216,8,128]{2,1,0:T(8,128)S(1)} all-gather(f32[27,8,128]{2,1,0:T(8,128)S(1)} %pad_maximum_fusion.1), channel_id=1, replica_groups=mesh['cluster'=64,'member'=8] {'member'}, dimensions={0}, use_global_device_ids=true | all-gather | bytes 995328 | tf_op jit(solution)/shard_map/all_gather | solution.py:125
  206.5 23.9 %while.58 = (s32[]{:T(128)}, f32[8,128]{1,0:T(8,128)S(1)}, f32[8,27648]{1,0:T(8,128)S(1)}, f32[3,27648]{1,0:T(4,128)S(1)}, f32[3,128]{1,0:T(4,128)S(1)}, /*index...) while((s32[]{:T(128)}, f32[8,128]{1,0:T(8,128)S(1)}, ...), condition=%wide.region_7.9_spmd.clone, body=%wide.region_6.8_spmd.clone.sunk | while | flops 13764617 | bytes 82645 | solution.py:64
  206.6 0.8 convolution_add_fusion.5
  207.4 0.8 convolution_add_fusion.5
  211.9 0.8 convolution_add_fusion.5
  212.8 0.8 convolution_add_fusion.5
  213.6 0.8 convolution_add_fusion.5
  217.2 0.8 convolution_add_fusion.5
  218.1 0.8 convolution_add_fusion.5
  218.9 0.8 convolution_add_fusion.5
  223.4 0.8 convolution_add_fusion.5
  224.3 0.8 convolution_add_fusion.5
  228.7 0.8 convolution_add_fusion.5
  229.6 0.8 convolution_add_fusion.5
  230.3 1.9 reduce.6
  232.7 1.7 copy.15
  234.4 2.5 %reshape.123 = f32[8,16384]{1,0:T(8,128)S(1)} reshape(f32[8,512,32]{2,1,0:T(8,128)} %copy.15) | data formatting | bytes 1048576 | tf_op jit(solution)/shard_map/reshape | solution.py:127
  237.0 10.0 %while.59 = (s32[]{:T(128)}, f32[8,128]{1,0:T(8,128)S(1)}, f32[8,16384]{1,0:T(8,128)S(1)}, f32[3,16384]{1,0:T(4,128)S(1)}, f32[3,128]{1,0:T(4,128)S(1)}, /*index...) while((s32[]{:T(128)}, f32[8,128]{1,0:T(8,128)S(1)}, ...), condition=%wide.region_9.11_spmd.clone, body=%wide.region_8.10_spmd.clone.sunk | while | flops 110102536 | bytes 570069 | solution.py:64
  237.3 4.8 %fusion.117 = f32[8,128]{1,0:T(8,128)S(1)} fusion(f32[128]{0:T(128)S(1)} %get-tuple-element.699, f32[8192]{0:T(1024)S(1)} %bitcast.108, f32[128]{0:T(128)S(1)} %get-tuple-element.701, f32[8192]{0:T(1024)S(1)} %bitcast.107, f32[128]{0:T(128)S(1)} %get-tuple-element.703, f32[8192]{0:T(1024)S(1)} %bitcast.106, f32[8,16384]{1,0:T(8,128)S(1)} %get-tuple-element.828, ...), kind=kOutput, calls=%fused_computation.97.clone.1 | convolution fusion | flops 110102528 | bytes 370181 | tf_op jit(solution)/shard_map/while/body/eval_jaxpr/dot_general | solution.py:59
  242.3 4.8 %fusion.117 = f32[8,128]{1,0:T(8,128)S(1)} fusion(f32[128]{0:T(128)S(1)} %get-tuple-element.699, f32[8192]{0:T(1024)S(1)} %bitcast.108, f32[128]{0:T(128)S(1)} %get-tuple-element.701, f32[8192]{0:T(1024)S(1)} %bitcast.107, f32[128]{0:T(128)S(1)} %get-tuple-element.703, f32[8192]{0:T(1024)S(1)} %bitcast.106, f32[8,16384]{1,0:T(8,128)S(1)} %get-tuple-element.828, ...), kind=kOutput, calls=%fused_computation.97.clone.1 | convolution fusion | flops 110102528 | bytes 370181 | tf_op jit(solution)/shard_map/while/body/eval_jaxpr/dot_general | solution.py:59
  (211 shorter events, 33.6 us)
Async XLA Ops:
  3.8 33.6 %all-to-all-start.1 = ((f32[64,3,128]{2,1,0:T(4,128)}), f32[64,3,128]{2,1,0:T(4,128)S(1)}, u32[]{:S(2)}, u32[]{:S(2)}) async-start(f32[64,3,128]{2,1,0:T(4,128)} %broadcast_select_fusion.2), calls=%async_computation.1 | async-start | bytes 262144 | tf_op jit(solution)/shard_map/all_to_all | solution.py:107
  24.0 22.3 %copy-start.5 = (pred[26]{0:T(512)(128)(4,1)}, pred[26]{0:T(512)(128)(4,1)S(1)}, u32[]{:S(2)}) copy-start(pred[26]{0:T(512)(128)(4,1)S(1)} %compare_and_fusion) | copy-start | bytes 82
  27.8 17.7 %copy-start.3 = (f32[3,128]{1,0:T(4,128)S(1)}, f32[3,128]{1,0:T(4,128)}, u32[]{:S(2)}) copy-start(f32[3,128]{1,0:T(4,128)} %param.20) | copy-start | bytes 4612
  27.8 17.8 %copy-start.1 = (f32[8,128]{1,0:T(8,128)S(1)}, f32[8,128]{1,0:T(8,128)}, u32[]{:S(2)}) copy-start(f32[8,128]{1,0:T(8,128)} %param.22) | copy-start | bytes 12292
  30.0 69.7 %copy-start.4 = (s32[1024]{0:T(1024)}, s32[1024]{0:T(1024)S(1)}, u32[]{:S(2)}) copy-start(s32[1024]{0:T(1024)S(1)} %pad_clamp_fusion.1) | copy-start | bytes 12292
  30.0 69.7 %copy-start = (f32[3,128]{1,0:T(4,128)S(1)}, f32[3,128]{1,0:T(4,128)}, u32[]{:S(2)}) copy-start(f32[3,128]{1,0:T(4,128)} %param.21) | copy-start | bytes 4612
  30.0 69.7 %copy-start.8 = (f32[8,128]{1,0:T(8,128)S(1)}, f32[8,128]{1,0:T(8,128)}, u32[]{:S(2)}) copy-start(f32[8,128]{1,0:T(8,128)} %custom-call) | copy-start | bytes 12292
  37.3 26.9 %all-to-all-start = ((f32[64,8,128]{2,1,0:T(8,128)}), f32[64,8,128]{2,1,0:T(8,128)S(1)}, u32[]{:S(2)}, u32[]{:S(2)}) async-start(f32[64,8,128]{2,1,0:T(8,128)} %broadcast_select_fusion.1), calls=%async_computation | async-start | bytes 524288 | tf_op jit(solution)/shard_map/all_to_all | solution.py:118
  64.2 59.4 %all-to-all-start.2 = ((f32[512,1,256]{2,1,0:T(1,128)}), f32[512,1,256]{2,1,0:T(1,128)S(1)}, u32[]{:S(2)}, u32[]{:S(2)}) async-start(f32[512,1,256]{2,1,0:T(1,128)} %reshape.157), calls=%async_computation.2 | async-start | bytes 1048576 | tf_op jit(solution)/shard_map/all_to_all | solution.py:128
  123.6 0.6 copy-start.9
  128.8 2.6 %copy-start.7 = (f32[8,128]{1,0:T(8,128)S(1)}, f32[8,128]{1,0:T(8,128)}, u32[]{:S(2)}) copy-start(f32[8,128]{1,0:T(8,128)} %custom-call.1) | copy-start | bytes 12292
  131.4 10.1 %copy-start.2 = (f32[8,128]{1,0:T(8,128)S(1)}, f32[8,128]{1,0:T(8,128)}, u32[]{:S(2)}) copy-start(f32[8,128]{1,0:T(8,128)} %param.23) | copy-start | bytes 12292
  131.5 10.1 %copy-start.10 = (f32[8,128]{1,0:T(8,128)S(1)}, f32[8,128]{1,0:T(8,128)}, u32[]{:S(2)}) copy-start(f32[8,128]{1,0:T(8,128)} %copy-done.9) | copy-start | bytes 12292
  131.5 10.1 %copy-start.11 = (f32[8]{0:T(128)S(1)}, f32[8]{0:T(128)}, u32[]{:S(2)}) copy-start(f32[8]{0:T(128)} %param.24) | copy-start | bytes 100
  142.5 33.1 %all-to-all-start.3 = ((f32[64,8,128]{2,1,0:T(8,128)}), f32[64,8,128]{2,1,0:T(8,128)S(1)}, u32[]{:S(2)}, u32[]{:S(2)}) async-start(f32[64,8,128]{2,1,0:T(8,128)} %broadcast_select_fusion), calls=%async_computation.3 | async-start | bytes 524288 | tf_op jit(solution)/shard_map/all_to_all | solution.py:118
  155.7 32.4 %copy-start.6 = (pred[26]{0:T(512)(128)(4,1)S(1)}, pred[26]{0:T(512)(128)(4,1)}, u32[]{:S(2)}) copy-start(pred[26]{0:T(512)(128)(4,1)} %copy-done.5) | copy-start | bytes 82
  175.6 54.8 %all-to-all-start.4 = ((f32[512,1,256]{2,1,0:T(1,128)}), f32[512,1,256]{2,1,0:T(1,128)S(1)}, u32[]{:S(2)}, u32[]{:S(2)}) async-start(f32[512,1,256]{2,1,0:T(1,128)} %reshape.159), calls=%async_computation.4 | async-start | bytes 1048576 | tf_op jit(solution)/shard_map/all_to_all | solution.py:128
